TPU v7x, 256 devices: a whole 4x4x8 slice. The times are simulated.
256 devices in a mesh: rep: 2 (over core), exp: 128 (over x, y, z).
Axes of the slice: x: 4, y: 4, z: 8, core: 2. Of those that a mesh axis runs over, the one named last changes fastest.
Arguments:
- attn_out: bfloat16 [16384, 4096], P(('rep', 'exp')), may hold values from -6 to 6
- out_weight: bfloat16 [4096, 2048], P('exp'), may hold values from -0.09375 to 0.09375
- router_weight: bfloat16 [2048, 128], replicated, may hold values from -0.125 to 0.125
- gate_weight: bfloat16 [128, 2048, 768], P('exp'), may hold values from -0.125 to 0.125
- up_weight: bfloat16 [128, 2048, 768], P('exp'), may hold values from -0.125 to 0.125
- down_weight: bfloat16 [128, 768, 2048], P('exp'), may hold values from -0.21875 to 0.21875
- cotangent: bfloat16 [16384, 2048], P(('rep', 'exp')), may hold values from -6 to 6
- log_ratios: float32 [16384], P(('rep', 'exp')), may hold values from -0.03 to 0.05
- expert_ids: int32 [16384, 8], P(('rep', 'exp')), may hold values from 0 to 127, as said below
- slot_ids: int32 [16384, 8], P(('rep', 'exp')), may hold values from 0 to 5, as said below
- episode_ids: int32 [16384], P(('rep', 'exp')), may hold values from 0 to 255, never falling along the last dimension, each value on 1 to 256 neighbouring positions
Outputs:
- token_grads: bfloat16 [16384, 4096], P(('rep', 'exp'))
- router_grad: float32 [2048, 128], P('exp')
Inputs may be any that keep to these rules, and one draw needn't show every extreme that they name: `expert_ids`: each row names 8 different experts. Among the rows of one device no expert is named more than 6 times, and on every device some expert is named exactly 6 times. `slot_ids`: among the rows of one device, the pairs of a row with one expert named in it get distinct slots; the slots of one expert on one device are 0 up to the number of its pairs there minus 1. `episode_ids`: episodes are runs of consecutive tokens, numbered in order; each has 1 to 256 tokens, one exactly 256.
All inputs are finite; a program needn't handle non-finite values.
Results may differ from a plain program's by a relative error of at most 0.012.
Values may be sent and summed in bfloat16 or wider, within the bound.
No kernel may reach another device: no remote copies, remote signals or barrier semaphores. Data moves between devices by JAX's collectives and lax.ppermute only.
A program may use at most 128 MiB of HBM per device.

v0:
```python
import jax
import jax.numpy as jnp
from jax import lax
from jax.sharding import PartitionSpec as P

clip_top = 4.0


def shards(
    attn_out,
    out_weight,
    router_weight,
    gate_weight,
    up_weight,
    down_weight,
    cotangent,
    log_ratios,
    expert_ids,
    slot_ids,
    episode_ids,
):
    tok_count = attn_out.shape[0]
    top_count = expert_ids.shape[1]
    model_width = cotangent.shape[1]
    expert_count = lax.axis_size("exp")
    device_count = lax.axis_size("rep") * expert_count
    capacity = 3 * tok_count * top_count // (2 * expert_count)
    episode_count = tok_count * device_count // 64
    episode_hits = (
        episode_ids[:, None] == jnp.arange(episode_count, dtype=jnp.int32)[None, :]
    ).astype(jnp.float32)
    part_logs = jnp.sum(episode_hits * log_ratios[:, None], axis=0)
    part_counts = jnp.sum(episode_hits, axis=0)
    log_sums, counts = lax.psum((part_logs, part_counts), ("rep", "exp"))
    episode_weight = jnp.minimum(jnp.exp(log_sums), clip_top)
    mean_weight = jnp.sum(counts * episode_weight) / (tok_count * device_count)
    token_scale = jnp.sum(episode_hits * episode_weight[None, :], axis=1) / mean_weight
    weight_full = lax.all_gather(out_weight, "exp", axis=0, tiled=True)
    hidden = jnp.dot(attn_out, weight_full, preferred_element_type=jnp.float32).astype(jnp.bfloat16)
    logits = jnp.dot(hidden, router_weight, preferred_element_type=jnp.float32)
    expert_hits = (expert_ids[:, :, None] == jnp.arange(expert_count, dtype=jnp.int32)).astype(
        jnp.float32
    )
    chosen = jnp.sum(expert_hits * logits[:, None, :], axis=2)
    raised = jnp.exp(chosen)
    gate_probs = raised / jnp.sum(raised, axis=1, keepdims=True)
    targets = expert_ids * capacity + slot_ids
    slot_count = expert_count * capacity
    labels = jnp.arange(tok_count, dtype=jnp.int32)[:, None] + 1
    matches = (targets[:, :, None] == jnp.arange(slot_count, dtype=jnp.int32)).astype(jnp.int32)
    owners = jnp.sum(matches * labels[:, :, None], axis=(0, 1))
    filled = owners > 0
    source_rows = jnp.maximum(owners - 1, 0)
    zero_value = jnp.zeros((), jnp.bfloat16)
    send_hidden = jnp.where(filled[:, None], hidden[source_rows], zero_value).reshape(
        expert_count, capacity, model_width
    )
    send_cot = jnp.where(filled[:, None], cotangent[source_rows], zero_value).reshape(
        expert_count, capacity, model_width
    )
    rows_in = lax.all_to_all(send_hidden, "exp", split_axis=0, concat_axis=0, tiled=True)
    cot_in = lax.all_to_all(send_cot, "exp", split_axis=0, concat_axis=0, tiled=True)
    gate_pre = jnp.einsum(
        "snd,df->snf", rows_in, gate_weight[0], preferred_element_type=jnp.float32
    )
    up_pre = jnp.einsum("snd,df->snf", rows_in, up_weight[0], preferred_element_type=jnp.float32)
    upstream = jnp.einsum("snd,fd->snf", cot_in, down_weight[0], preferred_element_type=jnp.float32)
    sigmoid_gate = jax.nn.sigmoid(gate_pre)
    slot_score = jnp.sum(upstream * (gate_pre * sigmoid_gate * up_pre), axis=2)
    grad_gate = (upstream * up_pre * sigmoid_gate * (1.0 + gate_pre * (1.0 - sigmoid_gate))).astype(
        jnp.bfloat16
    )
    grad_up = (upstream * gate_pre * sigmoid_gate).astype(jnp.bfloat16)
    back_rows = (
        jnp.einsum("snf,df->snd", grad_gate, gate_weight[0], preferred_element_type=jnp.float32)
        + jnp.einsum("snf,df->snd", grad_up, up_weight[0], preferred_element_type=jnp.float32)
    ).astype(jnp.bfloat16)
    back_home = lax.all_to_all(back_rows, "exp", split_axis=0, concat_axis=0, tiled=True)
    score_home = lax.all_to_all(slot_score, "exp", split_axis=0, concat_axis=0, tiled=True)
    pair_back = back_home.reshape(slot_count, model_width)[targets]
    pair_score = score_home.reshape(slot_count)[targets]
    mixed_back = jnp.sum(gate_probs[:, :, None] * pair_back.astype(jnp.float32), axis=1)
    logit_grad = gate_probs * (pair_score - jnp.sum(gate_probs * pair_score, axis=1, keepdims=True))
    full_grad = jnp.sum(expert_hits * logit_grad[:, :, None], axis=1)
    weighted = (token_scale[:, None] * full_grad).astype(jnp.bfloat16)
    router_part = jnp.einsum("td,te->de", hidden, weighted, preferred_element_type=jnp.float32)
    grad_hidden = (
        token_scale[:, None] * mixed_back
        + jnp.dot(weighted, router_weight.T, preferred_element_type=jnp.float32)
    ).astype(jnp.bfloat16)
    token_grads = jnp.dot(grad_hidden, weight_full.T, preferred_element_type=jnp.float32).astype(
        jnp.bfloat16
    )
    router_total = lax.psum(router_part, ("rep", "exp"))
    row_count = model_width // expert_count
    router_grad = lax.dynamic_slice_in_dim(
        router_total, lax.axis_index("exp") * row_count, row_count, 0
    )
    return (token_grads, router_grad)


def solution(mesh):
    placed = (
        P(("rep", "exp"), None),
        P("exp", None),
        P(),
        P("exp", None, None),
        P("exp", None, None),
        P("exp", None, None),
        P(("rep", "exp"), None),
        P(("rep", "exp")),
        P(("rep", "exp"), None),
        P(("rep", "exp"), None),
        P(("rep", "exp")),
    )
    return jax.shard_map(
        shards,
        mesh=mesh,
        in_specs=placed,
        out_specs=(P(("rep", "exp"), None), P("exp", None)),
        check_vma=False,
    )
```

profile of v0, /device:TPU:2, one launch (start us, length us, event | category | flops | bytes accessed | tf_op | source)
XLA Modules:
  0.0 948.8 jit_solution(6600559267684554942)
XLA Ops:
  9.3 4.3 gather_fusion
  13.5 6.3 gather.17
  19.8 144.6 %all-gather.2.cloned.1.call-done = bf16[4096,2048]{1,0:T(8,128)(2,1)} async-done(((bf16[32,2048]{1,0:T(8,128)(2,1)}), bf16[4096,2048]{1,0:T(8,128)(2,1)}) %all-gather.2.cloned.1.call-update) | async-done | bytes 16777232 | tf_op jit(solution)/shard_map/all_gather | solution.py:38
  164.4 9.0 convolution_convert_fusion.1
  173.4 4.3 gather_fusion.1
  177.7 6.2 gather.19
  184.0 5.2 broadcast_select_fusion.1
  189.2 106.0 %all_to_all.24 = bf16[128,6,2048]{2,1,0:T(8,128)(2,1)} all-to-all(bf16[128,6,2048]{2,1,0:T(8,128)(2,1)S(1)} %get-tuple-element.9), channel_id=1, replica_groups=mesh['rep'=2,'exp'=128] {'exp'}, dimensions={0} | all-to-all | bytes 6291456 | tf_op jit(solution)/shard_map/all_to_all | solution.py:61
  295.2 10.3 %all-to-all-start = ((bf16[128,6,2048]{2,1,0:T(8,128)(2,1)}), bf16[128,6,2048]{2,1,0:T(8,128)(2,1)}, u32[]{:S(2)}, u32[]{:S(2)}) async-start(bf16[128,6,2048]{2,1,0:T(8,128)(2,1)} %get-tuple-element.8), calls=%async_computation | async-start | bytes 8388608 | tf_op jit(solution)/shard_map/all_to_all | solution.py:62
  305.6 9.3 fusion.3
  314.9 7.5 fusion.6
  322.4 76.0 %all-to-all-done = bf16[128,6,2048]{2,1,0:T(8,128)(2,1)} async-done(((bf16[128,6,2048]{2,1,0:T(8,128)(2,1)}), bf16[128,6,2048]{2,1,0:T(8,128)(2,1)}, u32[]{:S(2)}, u32[]{:S(2)}) %all-to-all-start) | async-done | bytes 3145760 | tf_op jit(solution)/shard_map/all_to_all | solution.py:62
  398.5 11.8 %multiply_reduce_fusion = (f32[128,6]{0,1:T(8,128)S(1)}, f32[128,6,768]{2,0,1:T(8,128)}) fusion(f32[128,6,768]{2,0,1:T(8,128)} %fusion.6, f32[128,6,768]{2,0,1:T(8,128)} %fusion.3, bf16[1,768,2048]{2,1,0:T(8,128)(2,1)} %param.16, bf16[128,6,2048]{2,1,0:T(8,128)(2,1)} %all-to-all-done), kind=kOutput, calls=%fused_computation.20 | convolution fusion | flops 2420047104 | bytes 13372416 | tf_op jit(solution)/shard_map/snd,fd->snf/dot_general | solution.py:67
  411.1 8.7 all-to-all-start.3
  419.8 5.6 fusion.1
  428.3 3.7 copy.35
  432.1 14.4 %all-to-all-start.2 = ((bf16[128,6,2048]{2,1,0:T(8,128)(2,1)}), bf16[128,6,2048]{2,1,0:T(8,128)(2,1)}, u32[]{:S(2)}, u32[]{:S(2)}) async-start(bf16[128,6,2048]{2,1,0:T(8,128)(2,1)} %copy.35), calls=%async_computation.2 | async-start | bytes 8388608 | tf_op jit(solution)/shard_map/all_to_all | solution.py:78
  446.9 130.2 %psum.21 = f32[256]{0:T(256)S(1)} all-reduce(f32[256]{0:T(256)S(1)} %select_reduce_fusion.4), channel_id=1, replica_groups=mesh['rep'=2,'exp'=128] {'rep','exp'}, use_global_device_ids=true, to_apply=%region_1.0 | all-reduce | flops 256 | bytes 2048 | tf_op jit(solution)/shard_map/psum | solution.py:34
  577.3 74.9 %psum.22 = f32[256]{0:T(256)S(1)} all-reduce(f32[256]{0:T(256)S(1)} %get-tuple-element.2), channel_id=1, replica_groups=mesh['rep'=2,'exp'=128] {'rep','exp'}, use_global_device_ids=true, to_apply=%region_4.0 | all-reduce | flops 256 | bytes 2048 | tf_op jit(solution)/shard_map/psum | solution.py:34
  659.8 255.7 %all-reduce.2.cloned.1.call-done = f32[2048,128]{1,0:T(8,128)} async-done(((f32[2048,128]{1,0:T(8,128)}), f32[2048,128]{1,0:T(8,128)}) %all-reduce.2.cloned.1.call-update) | async-done | bytes 1048592 | tf_op jit(solution)/shard_map/psum | solution.py:94
  916.8 4.9 reshape.115
  921.7 3.3 gather_fusion.2
  925.0 4.2 fusion
  929.2 12.5 %convolution_convert_fusion = bf16[64,4096]{1,0:T(8,128)(2,1)} fusion(bf16[4096,2048]{1,0:T(8,128)(2,1)} %all-gather.2.cloned.1.call-done, bf16[2048,128]{1,0:T(8,128)(2,1)} %param.13, f32[64,2048]{1,0:T(8,128)} %fusion, f32[64]{0:T(128)S(1)} %broadcast_divide_fusion, f32[64,128]{1,0:T(8,128)S(1)} %select_reduce_fusion.1), kind=kOutput, calls=%fused_computation.5 | convolution fusion | flops 1107968000 | bytes 18383104 | tf_op jit(solution)/shard_map/dot_general | solution.py:91
  (62 shorter events, 14.4 us)
Async XLA Ops:
  7.2 298.4 %copy-start = (bf16[1,2048,768]{2,1,0:T(8,128)(2,1)S(1)}, bf16[1,2048,768]{2,1,0:T(8,128)(2,1)}, u32[]{:S(2)}) copy-start(bf16[1,2048,768]{2,1,0:T(8,128)(2,1)} %param.14) | copy-start | bytes 9437188
  7.2 2.1 copy-start.2
  7.2 157.2 %all-gather.2.cloned.1.call-start = ((), (), s32[]{:S(2)}) async-start(), calls=%async_computation.4 | async-start | bytes 16908288 | tf_op jit(solution)/shard_map/all_gather | solution.py:38
  295.2 103.3 %all-to-all-start = ((bf16[128,6,2048]{2,1,0:T(8,128)(2,1)}), bf16[128,6,2048]{2,1,0:T(8,128)(2,1)}, u32[]{:S(2)}, u32[]{:S(2)}) async-start(bf16[128,6,2048]{2,1,0:T(8,128)(2,1)} %get-tuple-element.8), calls=%async_computation | async-start | bytes 8388608 | tf_op jit(solution)/shard_map/all_to_all | solution.py:62
  305.5 9.4 copy-start.3
  305.5 9.4 copy-start.8
  411.1 21.0 %all-to-all-start.3 = ((f32[128,1,6]{2,1,0:T(1,128)}), f32[128,1,6]{2,1,0:T(1,128)S(1)}, u32[]{:S(2)}, u32[]{:S(2)}) async-start(f32[128,1,6]{2,1,0:T(1,128)} %copy.37), calls=%async_computation.3 | async-start | bytes 131072 | tf_op jit(solution)/shard_map/all_to_all | solution.py:79
  419.8 5.6 copy-start.9
  419.8 5.6 copy-start.10
  419.8 5.6 copy-start.11
  432.0 14.5 %copy-start.5 = (s32[64,8]{0,1:T(8,128)S(1)}, s32[64,8]{0,1:T(8,128)}, u32[]{:S(2)}) copy-start(s32[64,8]{0,1:T(8,128)} %param.19) | copy-start | bytes 6148
  432.0 14.8 %copy-start.6 = (s32[64]{0:T(128)S(1)}, s32[64]{0:T(128)}, u32[]{:S(2)}) copy-start(s32[64]{0:T(128)} %param.21) | copy-start | bytes 772
  432.0 14.8 %copy-start.7 = (f32[64]{0:T(128)S(1)}, f32[64]{0:T(128)}, u32[]{:S(2)}) copy-start(f32[64]{0:T(128)} %param.18) | copy-start | bytes 772
  432.1 221.4 %copy-start.4 = (bf16[2048,128]{1,0:T(8,128)(2,1)S(1)}, bf16[2048,128]{1,0:T(8,128)(2,1)}, u32[]{:S(2)}) copy-start(bf16[2048,128]{1,0:T(8,128)(2,1)} %param.13) | copy-start | bytes 1572868
  432.1 484.7 %all-to-all-start.2 = ((bf16[128,6,2048]{2,1,0:T(8,128)(2,1)}), bf16[128,6,2048]{2,1,0:T(8,128)(2,1)}, u32[]{:S(2)}, u32[]{:S(2)}) async-start(bf16[128,6,2048]{2,1,0:T(8,128)(2,1)} %copy.35), calls=%async_computation.2 | async-start | bytes 8388608 | tf_op jit(solution)/shard_map/all_to_all | solution.py:78
  446.5 469.0 %all-reduce.2.cloned.1.call-start = ((), (), s32[]{:S(2)}) async-start(), calls=%async_computation.5 | async-start | bytes 2097152 | tf_op jit(solution)/shard_map/psum | solution.py:94
  929.2 12.5 %copy-start.1 = (bf16[1,2048,768]{2,1,0:T(8,128)(2,1)S(1)}, bf16[1,2048,768]{2,1,0:T(8,128)(2,1)}, u32[]{:S(2)}) copy-start(bf16[1,2048,768]{2,1,0:T(8,128)(2,1)} %param.14) | copy-start | bytes 9437188
Sparse Core Ops, SparseCore 0:
  11.6 152.7 all-gather.1
  659.9 255.5 all-reduce.1
where the time goes:
time: 957 us; the launch traced here: 949 us
  waiting for transfers between devices  477 us (50%)
  blocking collectives  311 us (32%)
  matrix products  60.2 us (6%)
  local copies, waits for them, and re-layouts  38.7 us (4%)
  starting transfers between devices  33.5 us (4%)
  between operations  15.2 us (2%)
  other arithmetic  13 us (1%)
    psum x1, waiting for transfers between devices, shards(): router_total = lax.psum(router_part, ('rep', 'exp'))  256 us
    psum x2, blocking collectives, shards(): log_sums, counts = lax.psum((part_logs, part_counts), ('rep', 'exp'))  205 us
    all_gather x1, waiting for transfers between devices, shards(): weight_full = lax.all_gather(out_weight, 'exp', axis=0, tiled=True)  145 us
    all_to_all x1, blocking collectives, shards(): lax.all_to_all(send_hidden, 'exp', split_axis=0, concat_axis=0, tiled=True)  106 us
    all_to_all x1, waiting for transfers between devices, shards(): lax.all_to_all(send_cot, 'exp', split_axis=0, concat_axis=0, tiled=True)  76 us
  transfers between devices with their start and end apart: 5, of which 3 were waited for; matrix products, arithmetic and copies ran while one was open for 5% of the time, Pallas kernels for 0%

commit v1 on v0

--- a/solution.py
+++ b/solution.py
@@ -35,7 +35,10 @@
     episode_weight = jnp.minimum(jnp.exp(log_sums), clip_top)
     mean_weight = jnp.sum(counts * episode_weight) / (tok_count * device_count)
     token_scale = jnp.sum(episode_hits * episode_weight[None, :], axis=1) / mean_weight
-    weight_full = lax.all_gather(out_weight, "exp", axis=0, tiled=True)
+    size = lax.axis_size("exp")
+    blocks = jnp.stack([out_weight for _ in range(size)])
+    blocks = lax.all_to_all(blocks, "exp", split_axis=0, concat_axis=0)
+    weight_full = jnp.concatenate(blocks, axis=0)
     hidden = jnp.dot(attn_out, weight_full, preferred_element_type=jnp.float32).astype(jnp.bfloat16)
     logits = jnp.dot(hidden, router_weight, preferred_element_type=jnp.float32)
     expert_hits = (expert_ids[:, :, None] == jnp.arange(expert_count, dtype=jnp.int32)).astype(

time: 957 us -> 1210 us (1.26)
  waiting for transfers between devices: 477 us -> 686 us
  starting transfers between devices: 33.5 us -> 49.1 us
  local copies, waits for them, and re-layouts: 38.7 us -> 53.2 us
    all_to_all x0 -> x1, waiting for transfers between devices: none -> 353 us  [shards(): blocks = lax.all_to_all(blocks, 'exp', split_axis=0, concat_axis=0)]
    all_gather x1 -> x0, waiting for transfers between devices: 145 us -> none  [shards(): weight_full = lax.all_gather(out_weight, 'exp', axis=0, tiled=True)]
    all_to_all x0 -> x1, starting transfers between devices: none -> 16.1 us  [shards(): blocks = lax.all_to_all(blocks, 'exp', split_axis=0, concat_axis=0)]
  transfers between devices with their start and end apart: 5 -> 5, of which waited for: 3 -> 3; matrix products, arithmetic and copies ran while one was open for 5% -> 4% of each run, Pallas kernels for 0% -> 0%
where the time goes in v1:
time: 1210 us; the launch traced here: 1200 us
  waiting for transfers between devices  686 us (57%)
  blocking collectives  317 us (26%)
  matrix products  61.2 us (5%)
  local copies, waits for them, and re-layouts  53.2 us (4%)
  starting transfers between devices  49.1 us (4%)
  between operations  15.1 us (1%)
  other arithmetic  13.7 us (1%)
    all_to_all x1, waiting for transfers between devices, shards(): blocks = lax.all_to_all(blocks, 'exp', split_axis=0, concat_axis=0)  353 us
    psum x1, waiting for transfers between devices, shards(): router_total = lax.psum(router_part, ('rep', 'exp'))  256 us
    psum x2, blocking collectives, shards(): log_sums, counts = lax.psum((part_logs, part_counts), ('rep', 'exp'))  205 us
    all_to_all x1, blocking collectives, shards(): lax.all_to_all(send_hidden, 'exp', split_axis=0, concat_axis=0, tiled=True)  112 us
    all_to_all x1, waiting for transfers between devices, shards(): lax.all_to_all(send_cot, 'exp', split_axis=0, concat_axis=0, tiled=True)  77.2 us
  transfers between devices with their start and end apart: 5, of which 3 were waited for; matrix products, arithmetic and copies ran while one was open for 4% of the time, Pallas kernels for 0%

profile of v1, /device:TPU:2, one launch (start us, length us, event | category | flops | bytes accessed | tf_op | source)
XLA Modules:
  0.0 1195.7 jit_solution(7333654830277722228)
XLA Ops:
  7.2 6.9 stack.2
  14.1 16.1 %all-to-all-start = ((bf16[128,32,2048]{2,1,0:T(8,128)(2,1)}), bf16[128,32,2048]{2,1,0:T(8,128)(2,1)}, u32[]{:S(2)}, u32[]{:S(2)}) async-start(bf16[128,32,2048]{2,1,0:T(8,128)(2,1)} %stack.2), calls=%async_computation | async-start | bytes 33554432 | tf_op jit(solution)/shard_map/all_to_all | solution.py:40
  30.6 4.3 gather_fusion
  34.9 6.2 gather.17
  41.3 353.3 %all-to-all-done = bf16[128,32,2048]{2,1,0:T(8,128)(2,1)} async-done(((bf16[128,32,2048]{2,1,0:T(8,128)(2,1)}), bf16[128,32,2048]{2,1,0:T(8,128)(2,1)}, u32[]{:S(2)}, u32[]{:S(2)}) %all-to-all-start) | async-done | bytes 16777248 | tf_op jit(solution)/shard_map/all_to_all | solution.py:40
  394.6 9.0 convolution_convert_fusion.1
  403.6 4.3 gather_fusion.1
  407.9 6.2 gather.19
  414.1 5.3 broadcast_select_fusion.1
  419.4 112.2 %all_to_all.29 = bf16[128,6,2048]{2,1,0:T(8,128)(2,1)} all-to-all(bf16[128,6,2048]{2,1,0:T(8,128)(2,1)S(1)} %get-tuple-element.9), channel_id=1, replica_groups=mesh['rep'=2,'exp'=128] {'exp'}, dimensions={0} | all-to-all | bytes 6291456 | tf_op jit(solution)/shard_map/all_to_all | solution.py:64
  531.6 10.0 all-to-all-start.1
  541.6 9.4 fusion.3
  551.0 7.5 fusion.6
  558.5 77.2 %all-to-all-done.1 = bf16[128,6,2048]{2,1,0:T(8,128)(2,1)} async-done(((bf16[128,6,2048]{2,1,0:T(8,128)(2,1)}), bf16[128,6,2048]{2,1,0:T(8,128)(2,1)}, u32[]{:S(2)}, u32[]{:S(2)}) %all-to-all-start.1) | async-done | bytes 3145760 | tf_op jit(solution)/shard_map/all_to_all | solution.py:65
  635.7 11.9 multiply_reduce_fusion
  648.3 8.7 all-to-all-start.4
  657.0 5.6 fusion.1
  669.9 14.3 %all-to-all-start.3 = ((bf16[128,6,2048]{2,1,0:T(8,128)(2,1)}), bf16[128,6,2048]{2,1,0:T(8,128)(2,1)}, u32[]{:S(2)}, u32[]{:S(2)}) async-start(bf16[128,6,2048]{2,1,0:T(8,128)(2,1)} %copy.35), calls=%async_computation.3 | async-start | bytes 8388608 | tf_op jit(solution)/shard_map/all_to_all | solution.py:81
  684.6 130.9 %psum.21 = f32[256]{0:T(256)S(1)} all-reduce(f32[256]{0:T(256)S(1)} %select_reduce_fusion.4), channel_id=1, replica_groups=mesh['rep'=2,'exp'=128] {'rep','exp'}, use_global_device_ids=true, to_apply=%region_1.0 | all-reduce | flops 256 | bytes 2048 | tf_op jit(solution)/shard_map/psum | solution.py:34
  815.7 74.1 %psum.22 = f32[256]{0:T(256)S(1)} all-reduce(f32[256]{0:T(256)S(1)} %get-tuple-element.2), channel_id=1, replica_groups=mesh['rep'=2,'exp'=128] {'rep','exp'}, use_global_device_ids=true, to_apply=%region_4.0 | all-reduce | flops 256 | bytes 2048 | tf_op jit(solution)/shard_map/psum | solution.py:34
  901.3 255.7 %all-reduce.2.cloned.1.call-done = f32[2048,128]{1,0:T(8,128)} async-done(((f32[2048,128]{1,0:T(8,128)}), f32[2048,128]{1,0:T(8,128)}) %all-reduce.2.cloned.1.call-update) | async-done | bytes 1048592 | tf_op jit(solution)/shard_map/psum | solution.py:97
  1158.3 6.3 reshape.121
  1164.6 7.6 gather_fusion.2
  1176.4 12.3 %convolution_convert_fusion = bf16[64,4096]{1,0:T(8,128)(2,1)} fusion(bf16[4096,2048]{1,0:T(8,128)(2,1)} %bitcast, bf16[2048,128]{1,0:T(8,128)(2,1)} %param.13, f32[64,2048]{1,0:T(8,128)} %fusion, f32[64]{0:T(128)S(1)} %broadcast_divide_fusion, f32[64,128]{1,0:T(8,128)S(1)} %select_reduce_fusion.1), kind=kOutput, calls=%fused_computation.5 | convolution fusion | flops 1107968000 | bytes 18383104 | tf_op jit(solution)/shard_map/dot_general | solution.py:94
  (66 shorter events, 25.4 us)
Async XLA Ops:
  7.2 534.4 %copy-start = (bf16[1,2048,768]{2,1,0:T(8,128)(2,1)S(1)}, bf16[1,2048,768]{2,1,0:T(8,128)(2,1)}, u32[]{:S(2)}) copy-start(bf16[1,2048,768]{2,1,0:T(8,128)(2,1)} %param.14) | copy-start | bytes 9437188
  14.1 16.2 %copy-start.6 = (s32[64,8]{0,1:T(8,128)S(1)}, s32[64,8]{0,1:T(8,128)}, u32[]{:S(2)}) copy-start(s32[64,8]{0,1:T(8,128)} %param.19) | copy-start | bytes 6148
  14.1 16.2 %copy-start.7 = (s32[64,8]{0,1:T(8,128)S(1)}, s32[64,8]{0,1:T(8,128)}, u32[]{:S(2)}) copy-start(s32[64,8]{0,1:T(8,128)} %param.20) | copy-start | bytes 6148
  14.1 16.5 %copy-start.1 = (bf16[64,2048]{1,0:T(8,128)(2,1)S(1)}, bf16[64,2048]{1,0:T(8,128)(2,1)}, u32[]{:S(2)}) copy-start(bf16[64,2048]{1,0:T(8,128)(2,1)} %param.17) | copy-start | bytes 786436
  14.1 380.5 %all-to-all-start = ((bf16[128,32,2048]{2,1,0:T(8,128)(2,1)}), bf16[128,32,2048]{2,1,0:T(8,128)(2,1)}, u32[]{:S(2)}, u32[]{:S(2)}) async-start(bf16[128,32,2048]{2,1,0:T(8,128)(2,1)} %stack.2), calls=%async_computation | async-start | bytes 33554432 | tf_op jit(solution)/shard_map/all_to_all | solution.py:40
  531.6 104.1 %all-to-all-start.1 = ((bf16[128,6,2048]{2,1,0:T(8,128)(2,1)}), bf16[128,6,2048]{2,1,0:T(8,128)(2,1)}, u32[]{:S(2)}, u32[]{:S(2)}) async-start(bf16[128,6,2048]{2,1,0:T(8,128)(2,1)} %get-tuple-element.8), calls=%async_computation.1 | async-start | bytes 8388608 | tf_op jit(solution)/shard_map/all_to_all | solution.py:65
  541.6 9.4 copy-start.2
  541.6 9.4 copy-start.10
  648.3 21.0 %all-to-all-start.4 = ((f32[128,1,6]{2,1,0:T(1,128)}), f32[128,1,6]{2,1,0:T(1,128)S(1)}, u32[]{:S(2)}, u32[]{:S(2)}) async-start(f32[128,1,6]{2,1,0:T(1,128)} %copy.37), calls=%async_computation.4 | async-start | bytes 131072 | tf_op jit(solution)/shard_map/all_to_all | solution.py:82
  657.0 5.6 copy-start.11
  657.0 5.6 copy-start.12
  657.0 5.6 copy-start.13
  669.3 15.2 %copy-start.8 = (s32[64]{0:T(128)S(1)}, s32[64]{0:T(128)}, u32[]{:S(2)}) copy-start(s32[64]{0:T(128)} %param.21) | copy-start | bytes 772
  669.3 15.2 %copy-start.9 = (f32[64]{0:T(128)S(1)}, f32[64]{0:T(128)}, u32[]{:S(2)}) copy-start(f32[64]{0:T(128)} %param.18) | copy-start | bytes 772
  669.3 0.6 copy-start.5
  669.9 488.3 %all-to-all-start.3 = ((bf16[128,6,2048]{2,1,0:T(8,128)(2,1)}), bf16[128,6,2048]{2,1,0:T(8,128)(2,1)}, u32[]{:S(2)}, u32[]{:S(2)}) async-start(bf16[128,6,2048]{2,1,0:T(8,128)(2,1)} %copy.35), calls=%async_computation.3 | async-start | bytes 8388608 | tf_op jit(solution)/shard_map/all_to_all | solution.py:81
  684.2 472.8 %all-reduce.2.cloned.1.call-start = ((), (), s32[]{:S(2)}) async-start(), calls=%async_computation.5 | async-start | bytes 2097152 | tf_op jit(solution)/shard_map/psum | solution.py:97
  899.0 0.6 copy-start.3
  1164.6 7.6 copy-start.4
Sparse Core Ops, SparseCore 0:
  901.4 255.4 all-reduce.1
